TPU v7x, 32 devices: a whole 2x2x4 slice. The times are simulated.
32 devices in a mesh: slab: 8 (over z, y), sub: 4 (over x, core).
Axes of the slice: x: 2, y: 2, z: 4, core: 2. Of those that a mesh axis runs over, the one named last changes fastest.
Arguments:
- velocity: float32 [16384, 3, 128], P(('slab', 'sub')), may hold values from -6 to 6
- weight: float32 [16384, 128], P(('slab', 'sub')), may hold values from 0.2 to 2
- offset: int32 [16384, 128], P(('slab', 'sub')), may hold values from 0 to 127
- owner: int32 [16384, 1], P(('slab', 'sub')), may hold values from 0 to 31; in each aligned block of 512 rows (0 to 511, 512 to 1023, ...) at most 32 rows name the same one
- brick: int32 [16384, 1], P(('slab', 'sub')), may hold values from 0 to 4095
- flags: int32 [64, 256, 1024], P('slab', 'sub'), may hold values from 0 to 2, as said below
Outputs:
- updated: float32 [16384, 3, 128], P(('slab', 'sub'))
- pressure: float32 [64, 256, 1024], P('slab', 'sub')
- solved_face_velocity: float32 [3, 64, 256, 1024], P(None, 'slab', 'sub')
Inputs may be any that keep to these rules, and one draw needn't show every extreme that they name: Among the blocks of one device, at most 32 name the same owner. `flags`: 0 air, 1 liquid, 2 solid.
All inputs are finite; a program needn't handle non-finite values.
Results may differ from a plain program's by a relative error of at most 0.000075.
Values sent between devices are 32-bit elements; how exact they have to be, the bound alone decides.
A program may use at most 128 MiB of HBM per device.

v0:
```python
import functools

import jax
import jax.numpy as jnp
from jax import lax
from jax.experimental import pallas as pl
from jax.experimental.pallas import tpu as pltpu
from jax.sharding import PartitionSpec as P

LANES = 128
SUB = 8
ITERS = 3

step_size = 0.15
MESH = pl.DeviceIdType.MESH
F32 = jnp.float32
I32 = jnp.int32
VMEM_LIMIT = 60 * 1024 * 1024


def vmem():
    return pl.BlockSpec(memory_space=pltpu.VMEM)


def smem():
    return pl.BlockSpec(memory_space=pltpu.SMEM)


def anywhere():
    return pl.BlockSpec(memory_space=pl.ANY)


def struct(shape, dtype=F32):
    return jax.ShapeDtypeStruct(shape, dtype)


def shifted(block, axis, distance):
    devices = range(lax.axis_size(axis))
    route = [(i - distance, i) for i in devices if i - distance in devices]
    return lax.ppermute(block, axis, route)


def splat_kernel(devices, cap, vel, wgt, off, owner, brick, send, send_brick, slot, cnt, stage):
    @pl.loop(0, devices)
    def _(d):
        cnt[d] = 0

    @pl.loop(0, devices * cap)
    def _(s):
        send_brick[s] = -1

    cell = lax.broadcasted_iota(I32, (LANES, LANES), 0)

    @pl.loop(0, wgt.shape[0] // SUB)
    def _(group):
        base = pl.multiple_of(group * SUB, SUB)
        rows = pl.ds(base, SUB)
        w = wgt[rows, :]
        for c in range(4):
            value = w if c == 3 else vel[c, rows, :] * w
            high = value.astype(jnp.bfloat16).astype(F32)
            stage[c * SUB : (c + 1) * SUB, :] = high
            stage[(c + 4) * SUB : (c + 5) * SUB, :] = value - high
        for j in range(SUB):
            lhs = stage[pl.ds(j, SUB, stride=SUB), :].astype(jnp.bfloat16)
            where = off[pl.ds(base + j, 1), :]
            hit = (cell == where).astype(F32).astype(jnp.bfloat16)
            sums = lax.dot_general(
                lhs, hit, (((1,), (1,)), ((), ())), preferred_element_type=F32
            )
            sums = sums[0:4] + sums[4:8]
            o = owner[base + j]
            r = cnt[o]
            cnt[o] = r + 1
            send_brick[o * cap + r] = brick[base + j]
            slot[base + j] = o * (3 * cap) + r
            for c in range(4):
                send[pl.ds(o * (4 * cap) + c * cap + r, 1), :] = sums[c : c + 1]


def grid_kernel(devices, cap, arrived, brick, count, code, g_out, r_out, d_out, ex, ey, tot, prev, uy):
    x = pl.program_id(0)
    span_y = code.shape[1]
    chunk = 4

    @pl.when(x == 0)
    def _():
        piece = 128

        @pl.loop(0, tot.shape[1] // piece)
        def _(i):
            for c in range(4):
                tot[c, pl.ds(pl.multiple_of(i * piece, piece), piece), :] = jnp.zeros((piece, LANES), F32)

        prev[...] = jnp.zeros_like(prev)
        uy[0] = jnp.zeros((SUB, LANES), F32)

        @pl.loop(0, devices)
        def _(d):
            @pl.loop(0, count[d])
            def _(s):
                b = brick[d * cap + s]
                for c in range(4):
                    tot[c, pl.ds(b, 1), :] += arrived[pl.ds(d * (4 * cap) + c * cap + s, 1), :]

    lane = lax.broadcasted_iota(I32, (chunk, SUB, LANES), 2)

    @pl.loop(0, span_y // chunk)
    def _(k):
        y = k * chunk
        rows = pl.ds(pl.multiple_of((x * span_y + y) * SUB, SUB), chunk * SUB)
        strips = pl.ds(y, chunk)
        kind = code[0, strips]
        inverse = 1.0 / (tot[3, rows, :].reshape(chunk, SUB, LANES) + 1.0)
        moved = []
        for a in range(3):
            face = ((kind >> a) & 1).astype(F32)
            guess = tot[a, rows, :].reshape(chunk, SUB, LANES) * inverse
            g_out[a, 0, strips] = guess
            r_out[a, 0, strips] = face * inverse
            moved.append(face * guess)
        ux, v, uz = moved
        uy[pl.ds(y + 1, chunk)] = v
        turned = pltpu.roll(uz, 1, 2)
        before = jnp.where(lane == 0, pltpu.roll(turned, 1, 1), turned)
        spread = ux - prev[strips]
        spread = spread + (v - uy[strips])
        spread = spread + (uz - before)
        d_out[0, strips] = spread
        prev[strips] = ux

    ey[0, 0] = uy[span_y]
    ex[...] = prev[...]


def solve_kernel(
    devices, cap, g_hbm, r_hbm, d_hbm, k_hbm, ex_hbm, ey_hbm, brick, p_out, reply,
    rx, ry, rz, div, kind, g, hx, hy, p1, p2, p3, here, out_sem, send_sem, recv_sem,
):
    span_x, span_y = div.shape[0], div.shape[1]
    chunk = 4
    n_slab, n_sub = lax.axis_size("slab"), lax.axis_size("sub")
    slab, sub = lax.axis_index("slab"), lax.axis_index("sub")
    east, west = lax.rem(slab + 1, n_slab), lax.rem(slab + n_slab - 1, n_slab)
    north, south = lax.rem(sub + 1, n_sub), lax.rem(sub + n_sub - 1, n_sub)
    locals_ = [
        pltpu.make_async_copy(src, dst, here.at[i])
        for i, (src, dst) in enumerate(
            [
                (d_hbm, div),
                (k_hbm, kind),
                (r_hbm.at[0], rx.at[pl.ds(1, span_x)]),
                (r_hbm.at[1], ry.at[:, pl.ds(1, span_y)]),
                (r_hbm.at[2], rz),
                (g_hbm, g),
            ]
        )
    ]
    for copy in locals_:
        copy.start()
    barrier = pltpu.get_barrier_semaphore()
    for axis, peer in (("slab", east), ("slab", west), ("sub", north), ("sub", south)):
        pl.semaphore_signal(barrier, inc=1, device_id={axis: peer}, device_id_type=MESH)
    pl.semaphore_wait(barrier, 4)

    def remote(index, src, dst, axis, peer):
        return pltpu.make_async_remote_copy(
            src_ref=src, dst_ref=dst, send_sem=send_sem.at[index], recv_sem=recv_sem.at[index],
            device_id={axis: peer}, device_id_type=MESH,
        )

    edges = [
        remote(0, ex_hbm, hx, "slab", east),
        remote(1, ey_hbm.at[:, 0], hy, "sub", north),
        remote(2, r_hbm.at[0, span_x - 1], rx.at[0], "slab", east),
        remote(3, r_hbm.at[1, :, span_y - 1], ry.at[:, 0], "sub", north),
    ]
    for copy in edges:
        copy.start()

    xs, ys = pl.ds(1, span_x), pl.ds(1, span_y)

    def x_halo(field, first, both):
        copies = [remote(first, field.at[1, ys], field.at[span_x + 1, ys], "slab", west)]
        if both:
            copies.append(remote(first + 1, field.at[span_x, ys], field.at[0, ys], "slab", east))
        return copies

    def y_halo(field, first, both):
        copies = [remote(first, field.at[xs, 1], field.at[xs, span_y + 1], "sub", south)]
        if both:
            copies.append(remote(first + 1, field.at[xs, span_y], field.at[xs, 0], "sub", north))
        return copies

    lane = lax.broadcasted_iota(I32, (chunk, SUB, LANES), 2)

    def onward(value):
        turned = pltpu.roll(value, LANES - 1, 2)
        return jnp.where(lane == LANES - 1, pltpu.roll(turned, SUB - 1, 1), turned)

    def back(value):
        turned = pltpu.roll(value, 1, 2)
        return jnp.where(lane == 0, pltpu.roll(turned, 1, 1), turned)

    def layer(x, body):
        @pl.loop(0, span_y // chunk)
        def _(k):
            body(x, k * chunk)

    def sweep(field, body, first, both):
        layer(0, body)
        layer(span_x - 1, body)
        copies = x_halo(field, first, both)
        for copy in copies:
            copy.start()

        @pl.loop(1, span_x - 1)
        def _(x):
            layer(x, body)

        later = y_halo(field, first + 2, both)
        for copy in later:
            copy.start()
        for copy in copies + later:
            copy.wait()

    def lifted(x, y, raised):
        wet = kind[x, pl.ds(y, chunk)] >= 8
        return jnp.where(wet, jnp.maximum(raised, 0.0), 0.0)

    for i in (0, 1):
        locals_[i].wait()
    for copy in edges:
        copy.wait()
    first_x = (slab > 0).astype(F32)
    first_y = (sub > 0).astype(F32)

    @pl.loop(0, span_y)
    def _(y):
        div[0, y] = div[0, y] - first_x * hx[y]
        rx[0, y] = first_x * rx[0, y]

    @pl.loop(0, span_x)
    def _(x):
        div[x, 0] = div[x, 0] - first_y * hy[x]
        ry[x, 0] = first_y * ry[x, 0]

    def start(x, y):
        p1[x + 1, pl.ds(y + 1, chunk)] = lifted(x, y, -step_size * div[x, pl.ds(y, chunk)])

    sweep(p1, start, 4, True)
    for i in (2, 3, 4):
        locals_[i].wait()

    def ascend(old, new):
        def body(x, y):
            strips, inner = pl.ds(y, chunk), pl.ds(y + 1, chunk)
            p = old[x + 1, inner]
            flow = rz[x, strips] * (p - onward(p))
            spread = div[x, strips] + (flow - back(flow))
            spread = spread + rx[x + 1, strips] * (p - old[x + 2, inner])
            spread = spread - rx[x, strips] * (old[x, inner] - p)
            spread = spread + ry[x, inner] * (p - old[x + 1, pl.ds(y + 2, chunk)])
            spread = spread - ry[x, strips] * (old[x + 1, strips] - p)
            new[x + 1, inner] = lifted(x, y, p - step_size * spread)

        return body

    sweep(p2, ascend(p1, p2), 8, True)
    sweep(p3, ascend(p2, p3), 12, False)
    locals_[5].wait()
    leave = pltpu.make_async_copy(p3, p_out, out_sem)
    leave.start()

    @pl.loop(0, span_x)
    def _(x):
        def body(x, y):
            strips, inner = pl.ds(y, chunk), pl.ds(y + 1, chunk)
            p = p3[x + 1, inner]
            after = (p3[x + 2, inner], p3[x + 1, pl.ds(y + 2, chunk)], onward(p))
            link = (rx[x + 1, strips], ry[x, inner], rz[x, strips])
            for a in range(3):
                shut = jnp.where(link[a] > 0.0, 0.0, -g[a, x, strips])
                g[a, x, strips] = shut + link[a] * (p - after[a])

        layer(x, body)

    per_layer = span_y * SUB

    @pl.loop(0, devices)
    def _(d):
        @pl.loop(0, cap)
        def _(s):
            b = jnp.maximum(brick[d * cap + s], 0)
            for a in range(3):
                row = g[a, b // per_layer, (b // SUB) % span_y, pl.ds(b % SUB, 1), :]
                reply[d * 3 + a, pl.ds(s, 1), :] = row

    leave.wait()


def face_kernel(g, r, p_here, p_next, u_out, p_out, stage):
    span_y = g.shape[2]
    lane = lax.broadcasted_iota(I32, (SUB, SUB, LANES), 2)

    @pl.loop(0, span_y // SUB)
    def _(k):
        y = pl.multiple_of(k * SUB, SUB)
        strips, inner = pl.ds(y, SUB), pl.ds(y + 1, SUB)
        p = p_here[0, inner]
        turned = pltpu.roll(p, LANES - 1, 2)
        up = jnp.where(lane == LANES - 1, pltpu.roll(turned, SUB - 1, 1), turned)
        after = (p_next[0, inner], p_here[0, pl.ds(y + 2, SUB)], up)
        stage[3] = p.reshape(SUB * SUB, LANES)
        for a in range(3):
            link = r[a, 0, strips]
            face = jnp.where(link > 0.0, g[a, 0, strips] + link * (p - after[a]), 0.0)
            stage[a] = face.reshape(SUB * SUB, LANES)
        for z in range(SUB):
            cols = slice(z * LANES, (z + 1) * LANES)
            pick = pl.ds(z, SUB, stride=SUB)
            p_out[0, strips, cols] = stage[3, pick, :]
            for a in range(3):
                u_out[a, 0, strips, cols] = stage[a, pick, :]


def gather_kernel(cap, vel, off, slot, back, out, stage):
    @pl.loop(0, off.shape[0] // SUB)
    def _(group):
        base = pl.multiple_of(group * SUB, SUB)
        rows = pl.ds(base, SUB)
        for j in range(SUB):
            s = slot[base + j]
            for c in range(3):
                stage[pl.ds(c * SUB + j, 1), :] = back[pl.ds(s + c * cap, 1), :]
        where = off[rows, :]
        for c in range(3):
            picked = jnp.take_along_axis(
                stage[c * SUB : (c + 1) * SUB, :], where, axis=1, mode="promise_in_bounds"
            )
            out[c, rows, :] = vel[c, rows, :] + picked


def on_device(velocity, weight, offset, owner, brick, flags):
    devices = lax.axis_size("slab") * lax.axis_size("sub")
    blocks = velocity.shape[0]
    cap = 2 * blocks // devices
    span_x, span_y, span_z = flags.shape
    bricks = span_x * span_y * span_z // LANES
    params = functools.partial(pltpu.CompilerParams, vmem_limit_bytes=VMEM_LIMIT)
    vel = velocity.transpose(1, 0, 2)
    grid4 = (span_x, span_y, SUB, LANES)

    open_cell = (flags != 2).astype(F32)
    wall_x = shifted(open_cell[:1], "slab", -1)
    wall_y = shifted(open_cell[:, :1], "sub", -1)

    send, send_brick, slot = pl.pallas_call(
        functools.partial(splat_kernel, devices, cap),
        out_shape=(
            struct((devices * 4 * cap, LANES)),
            struct((devices * cap,), I32),
            struct((blocks,), I32),
        ),
        in_specs=[vmem(), vmem(), vmem(), smem(), smem()],
        out_specs=(vmem(), smem(), smem()),
        scratch_shapes=[pltpu.SMEM((devices,), I32), pltpu.VMEM((8 * SUB, LANES), F32)],
        compiler_params=params(),
        name="splat",
    )(vel, weight, offset, owner[:, 0], brick[:, 0])

    exchange = functools.partial(
        lax.all_to_all, axis_name=("slab", "sub"), split_axis=0, concat_axis=0, tiled=True
    )
    arrived_brick = exchange(send_brick.reshape(devices, cap))
    arrived = exchange(send.reshape(devices, 4 * cap, LANES))
    count = jnp.sum((arrived_brick >= 0).astype(I32), axis=1)
    arrived_brick = arrived_brick.reshape(devices * cap)

    is_open = flags != 2
    next_x = jnp.concatenate([is_open[1:], wall_x > 0.0], 0)
    next_y = jnp.concatenate([is_open[:, 1:], wall_y > 0.0], 1)
    next_z = jnp.concatenate([is_open[:, :, 1:], jnp.zeros((span_x, span_y, 1), bool)], 2)
    code = (
        (is_open & next_x).astype(I32)
        + 2 * (is_open & next_y).astype(I32)
        + 4 * (is_open & next_z).astype(I32)
        + 8 * (flags == 1).astype(I32)
    ).reshape(grid4)

    whole = lambda *shape: pl.BlockSpec(shape, lambda x: (0,) * len(shape))
    one_layer = pl.BlockSpec((1, span_y, SUB, LANES), lambda x: (x, 0, 0, 0))
    three = pl.BlockSpec((3, 1, span_y, SUB, LANES), lambda x: (0, x, 0, 0, 0))
    g, r, div, edge_x, edge_y = pl.pallas_call(
        functools.partial(grid_kernel, devices, cap),
        grid=(span_x,),
        out_shape=(
            struct((3,) + grid4),
            struct((3,) + grid4),
            struct(grid4),
            struct((span_y, SUB, LANES)),
            struct((span_x, 1, SUB, LANES)),
        ),
        in_specs=[whole(devices * 4 * cap, LANES), smem(), smem(), one_layer],
        out_specs=(
            three,
            three,
            one_layer,
            whole(span_y, SUB, LANES),
            pl.BlockSpec((1, 1, SUB, LANES), lambda x: (x, 0, 0, 0)),
        ),
        scratch_shapes=[
            pltpu.VMEM((4, bricks, LANES), F32),
            pltpu.VMEM((span_y, SUB, LANES), F32),
            pltpu.VMEM((span_y + 1, SUB, LANES), F32),
        ],
        compiler_params=params(dimension_semantics=("arbitrary",)),
        name="grid",
    )(arrived.reshape(devices * 4 * cap, LANES), arrived_brick, count, code)

    padded = (span_x + 2, span_y + 2, SUB, LANES)
    p, reply = pl.pallas_call(
        functools.partial(solve_kernel, devices, cap),
        out_shape=(struct(padded), struct((devices * 3, cap, LANES))),
        in_specs=[anywhere()] * 6 + [smem()],
        out_specs=(anywhere(), vmem()),
        scratch_shapes=[
            pltpu.VMEM((span_x + 1, span_y, SUB, LANES), F32),
            pltpu.VMEM((span_x, span_y + 1, SUB, LANES), F32),
            pltpu.VMEM(grid4, F32),
            pltpu.VMEM(grid4, F32),
            pltpu.VMEM(grid4, I32),
            pltpu.VMEM((3,) + grid4, F32),
            pltpu.VMEM((span_y, SUB, LANES), F32),
            pltpu.VMEM((span_x, SUB, LANES), F32),
            pltpu.VMEM(padded, F32),
            pltpu.VMEM(padded, F32),
            pltpu.VMEM(padded, F32),
            pltpu.SemaphoreType.DMA((6,)),
            pltpu.SemaphoreType.DMA,
            pltpu.SemaphoreType.DMA((16,)),
            pltpu.SemaphoreType.DMA((16,)),
        ],
        compiler_params=params(collective_id=0, has_side_effects=True),
        name="solve",
    )(g, r, div, code, edge_x, edge_y, arrived_brick)

    returned = exchange(reply.reshape(devices, 3 * cap, LANES))

    solved, pressure = pl.pallas_call(
        face_kernel,
        grid=(span_x,),
        out_shape=(struct((3,) + flags.shape), struct(flags.shape)),
        in_specs=[
            three,
            three,
            pl.BlockSpec((1, span_y + 2, SUB, LANES), lambda x: (x + 1, 0, 0, 0)),
            pl.BlockSpec((1, span_y + 2, SUB, LANES), lambda x: (x + 2, 0, 0, 0)),
        ],
        out_specs=(
            pl.BlockSpec((3, 1, span_y, span_z), lambda x: (0, x, 0, 0)),
            pl.BlockSpec((1, span_y, span_z), lambda x: (x, 0, 0)),
        ),
        scratch_shapes=[pltpu.VMEM((4, SUB * SUB, LANES), F32)],
        compiler_params=params(dimension_semantics=("arbitrary",)),
        cost_estimate=pl.CostEstimate(flops=10**7, bytes_accessed=24 * 10**6, transcendentals=0),
        name="faces",
    )(g, r, p, p)

    updated = pl.pallas_call(
        functools.partial(gather_kernel, cap),
        out_shape=struct((3, blocks, LANES)),
        in_specs=[vmem(), vmem(), smem(), vmem()],
        out_specs=vmem(),
        scratch_shapes=[pltpu.VMEM((3 * SUB, LANES), F32)],
        compiler_params=params(),
        name="gather",
    )(vel, offset, slot, returned.reshape(devices * 3 * cap, LANES))
    return updated.transpose(1, 0, 2), pressure, solved


def solution(mesh):
    in_specs = (
        P(("slab", "sub"), None, None),
        P(("slab", "sub"), None),
        P(("slab", "sub"), None),
        P(("slab", "sub"), None),
        P(("slab", "sub"), None),
        P("slab", "sub", None),
    )
    out_specs = (
        P(("slab", "sub"), None, None),
        P("slab", "sub", None),
        P(None, "slab", "sub", None),
    )
    return jax.shard_map(
        on_device, mesh=mesh, in_specs=in_specs, out_specs=out_specs, check_vma=False
    )
```

profile of v0, /device:TPU:0, one launch (start us, length us, event | category | flops | bytes accessed | tf_op | source)
XLA Modules:
  0.0 278.0 jit_solution(15439140031428504698)
XLA Ops:
  0.6 25.6 %splat.1 = (f32[4096,128]{1,0:T(8,128)}, s32[1024]{0:T(1024)}, s32[512]{0:T(512)}) custom-call(f32[3,512,128]{2,1,0:T(8,128)} %bitcast.17, f32[512,128]{1,0:T(8,128)} %wgt.1, s32[512,128]{1,0:T(8,128)} %off.3, s32[512]{0:T(512)} %bitcast.23, s32[512]{0:T(512)} %bitcast.24), custom_call_target="tpu_custom_call" | custom-call | tf_op jit(solution)/shard_map/splat/pallas_call | solution.py:358
  26.3 0.8 all_to_all.13
  27.1 14.3 %all_to_all.19 = s32[32,1,32]{2,1,0:T(1,128)S(1)} all-to-all(s32[32,1,32]{2,1,0:T(1,128)S(1)} %all_to_all.13), channel_id=1, replica_groups=mesh['slab'=8,'sub'=4] {'slab','sub'}, dimensions={0} | all-to-all | bytes 8192 | tf_op jit(solution)/shard_map/all_to_all | solution.py:375
  41.4 3.6 %all-to-all-start = ((f32[32,128,128]{2,1,0:T(8,128)}), f32[32,128,128]{2,1,0:T(8,128)}, u32[]{:S(2)}, u32[]{:S(2)}) async-start(f32[32,128,128]{2,1,0:T(8,128)} %bitcast.19), calls=%async_computation | async-start | bytes 4194304 | tf_op jit(solution)/shard_map/all_to_all | solution.py:376
  45.4 0.7 slice.21
  46.1 1.3 collective-permute-start
  47.5 1.3 collective-permute-start.1
  48.8 0.8 slice.20
  49.9 1.4 slice.24
  51.3 0.7 convert_reduce_fusion.count
  52.0 0.6 broadcast.20
  52.6 0.7 reduce.4
  53.3 0.7 reshape.34.brick
  54.0 13.7 %collective-permute-done = f32[1,64,1024]{2,1,0:T(8,128)S(1)} collective-permute-done((f32[1,64,1024]{2,1,0:T(8,128)}, f32[1,64,1024]{2,1,0:T(8,128)S(1)}, u32[]{:S(2)}, u32[]{:S(2)}) %collective-permute-start) | collective-permute-done | bytes 262176 | tf_op jit(solution)/shard_map/ppermute | solution.py:40
  67.7 2.3 select_add_fusion
  70.1 1.8 copy.11
  71.8 22.5 %all-to-all-done = f32[32,128,128]{2,1,0:T(8,128)} async-done(((f32[32,128,128]{2,1,0:T(8,128)}), f32[32,128,128]{2,1,0:T(8,128)}, u32[]{:S(2)}, u32[]{:S(2)}) %all-to-all-start) | async-done | bytes 2097184 | tf_op jit(solution)/shard_map/all_to_all | solution.py:376
  94.4 23.9 %grid.1 = (f32[3,8,64,8,128]{4,3,2,1,0:T(8,128)}, f32[3,8,64,8,128]{4,3,2,1,0:T(8,128)}, f32[8,64,8,128]{3,2,1,0:T(8,128)}, f32[64,8,128]{2,1,0:T(8,128)}, f32[8,1,8,128]{3,2,1,0:T(8,128)}) custom-call(f32[4096,128]{1,0:T(8,128)} %bitcast.4.arrived, s32[1024]{0:T(1024)} %reshape.34.brick, s32[32]{0:T(128)} %convert_reduce_fusion.count, ...), custom_call_target="tpu_custom_call" | custom-call | tf_op jit(solution)/shard_map/grid/pallas_call | solution.py:394
  118.3 100.7 %solve.1 = (f32[10,66,8,128]{3,2,1,0:T(8,128)}, f32[96,32,128]{2,1,0:T(8,128)}) custom-call(f32[3,8,64,8,128]{4,3,2,1,0:T(8,128)} %get-tuple-element.18.g_hbm.g, f32[3,8,64,8,128]{4,3,2,1,0:T(8,128)} %get-tuple-element.19.r_hbm.r, f32[8,64,8,128]{3,2,1,0:T(8,128)} %get-tuple-element.20.d_hbm, s32[8,64,8,128]{3,2,1,0:T(8,128)} %bitcast.14, ...), custom_call_target="tpu_custom_call" | custom-call | tf_op jit(solution)/shard_map/solve/pallas_call | solution.py:422
  219.0 11.8 %all-to-all-start.2 = ((f32[32,96,128]{2,1,0:T(8,128)}), f32[32,96,128]{2,1,0:T(8,128)S(1)}, u32[]{:S(2)}, u32[]{:S(2)}) async-start(f32[32,96,128]{2,1,0:T(8,128)} %bitcast.20), calls=%async_computation.2 | async-start | bytes 3145728 | tf_op jit(solution)/shard_map/all_to_all | solution.py:448
  230.8 13.1 %faces.1 = (f32[3,8,64,1024]{3,2,1,0:T(8,128)}, f32[8,64,1024]{2,1,0:T(8,128)}) custom-call(f32[3,8,64,8,128]{4,3,2,1,0:T(8,128)} %get-tuple-element.18.g_hbm.g, f32[3,8,64,8,128]{4,3,2,1,0:T(8,128)} %get-tuple-element.19.r_hbm.r, f32[10,66,8,128]{3,2,1,0:T(8,128)} %get-tuple-element.24.p_here.p_next, f32[10,66,8,128]{3,2,1,0:T(8,128)} %get-tuple-element.24.p_here.p_next), custom_call_target="tpu_custom_call" | custom-call | flops 10000000 | bytes 24000000 | tf_op jit(solution)/shard_map/faces/pallas_call | solution.py:450
  243.9 24.6 %all-to-all-done.2 = f32[32,96,128]{2,1,0:T(8,128)S(1)} async-done(((f32[32,96,128]{2,1,0:T(8,128)}), f32[32,96,128]{2,1,0:T(8,128)S(1)}, u32[]{:S(2)}, u32[]{:S(2)}) %all-to-all-start.2) | async-done | bytes 1572896 | tf_op jit(solution)/shard_map/all_to_all | solution.py:448
  268.5 1.1 copy-done.1
  269.6 8.4 %gather.1 = f32[3,512,128]{2,1,0:T(8,128)} custom-call(f32[3,512,128]{2,1,0:T(8,128)} %bitcast.18, s32[512,128]{1,0:T(8,128)} %off.3, s32[512]{0:T(512)} %get-tuple-element.15.slot, f32[3072,128]{1,0:T(8,128)} %bitcast.16), custom_call_target="tpu_custom_call" | custom-call | tf_op jit(solution)/shard_map/gather/pallas_call | solution.py:470
  (9 shorter events, 0.9 us)
Async XLA Ops:
  41.4 3.6 %copy-start = (s32[8,64,1024]{2,1,0:T(8,128)S(1)}, s32[8,64,1024]{2,1,0:T(8,128)}, u32[]{:S(2)}) copy-start(s32[8,64,1024]{2,1,0:T(8,128)} %param.11) | copy-start | bytes 6291460
  41.4 53.0 %all-to-all-start = ((f32[32,128,128]{2,1,0:T(8,128)}), f32[32,128,128]{2,1,0:T(8,128)}, u32[]{:S(2)}, u32[]{:S(2)}) async-start(f32[32,128,128]{2,1,0:T(8,128)} %bitcast.19), calls=%async_computation | async-start | bytes 4194304 | tf_op jit(solution)/shard_map/all_to_all | solution.py:376
  46.1 21.5 %collective-permute-start = (f32[1,64,1024]{2,1,0:T(8,128)}, f32[1,64,1024]{2,1,0:T(8,128)S(1)}, u32[]{:S(2)}, u32[]{:S(2)}) collective-permute-start(f32[1,64,1024]{2,1,0:T(8,128)} %slice.21), channel_id=1, source_target_pairs={{4,0},{8,4},{12,8},{16,12},{20,16},{24,20},{28,24},{5,1},{9,5},{13... | collective-permute-start | bytes 786440 | tf_op jit(solution)/shard_map/ppermute | solution.py:40
  47.5 6.5 %collective-permute-start.1 = (f32[8,1,1024]{2,1,0:T(1,128)S(1)}, f32[8,1,1024]{2,1,0:T(1,128)S(1)}, u32[]{:S(2)}, u32[]{:S(2)}) collective-permute-start(f32[8,1,1024]{2,1,0:T(1,128)S(1)} %slice.23), channel_id=1, source_target_pairs={{1,0},{2,1},{3,2},{5,4},{6,5},{7,6},{9,8},{10,9},{11,10},{13,12},{... | collective-permute-start | bytes 98312 | tf_op jit(solution)/shard_map/ppermute | solution.py:40
  219.0 49.5 %all-to-all-start.2 = ((f32[32,96,128]{2,1,0:T(8,128)}), f32[32,96,128]{2,1,0:T(8,128)S(1)}, u32[]{:S(2)}, u32[]{:S(2)}) async-start(f32[32,96,128]{2,1,0:T(8,128)} %bitcast.20), calls=%async_computation.2 | async-start | bytes 3145728 | tf_op jit(solution)/shard_map/all_to_all | solution.py:448
  268.5 1.1 copy-start.1
where the time goes:
time: 278 us
  Pallas kernels  172 us (62%)
  waiting for transfers between devices  60.8 us (22%)
  starting transfers between devices  18 us (6%)
  blocking collectives  14.3 us (5%)
  local copies, waits for them, and re-layouts  8.25 us (3%)
  other arithmetic  4.21 us (2%)
    pallas_call x1, Pallas kernels, on_device(): pl.pallas_call(functools.partial(solve_kernel, devices, cap), out_shape=(...  101 us
    pallas_call x1, Pallas kernels, on_device(): pl.pallas_call(functools.partial(splat_kernel, devices, cap), out_shape=(...  25.6 us
    all_to_all x1, waiting for transfers between devices, on_device(): returned = exchange(reply.reshape(devices, 3 * cap, LANES))  24.6 us
    pallas_call x1, Pallas kernels, on_device(): pl.pallas_call(functools.partial(grid_kernel, devices, cap), grid=(span_x...  23.9 us
    all_to_all x1, waiting for transfers between devices, on_device(): arrived = exchange(send.reshape(devices, 4 * cap, LANES))  22.5 us
    all_to_all x1, blocking collectives, on_device(): arrived_brick = exchange(send_brick.reshape(devices, cap))  14.3 us
    ppermute x2, waiting for transfers between devices, shifted(): return lax.ppermute(block, axis, route)  13.7 us
    pallas_call x1, Pallas kernels, on_device(): pl.pallas_call(face_kernel, grid=(span_x,), out_shape=(struct((3,) + flag...  13.1 us
  transfers between devices with their start and end apart: 4, of which 3 were waited for; matrix products, arithmetic and copies ran while one was open for 4% of the time, Pallas kernels for 5%

commit v1 on v0

--- a/solution.py
+++ b/solution.py
@@ -40,15 +40,19 @@
     return lax.ppermute(block, axis, route)
 
 
-def splat_kernel(devices, cap, vel, wgt, off, owner, brick, send, send_brick, slot, cnt, stage):
+def splat_kernel(devices, cap, vel, wgt, off, owner, brick, send, slot, cnt, stage):
     @pl.loop(0, devices)
     def _(d):
         cnt[d] = 0
 
-    @pl.loop(0, devices * cap)
-    def _(s):
-        send_brick[s] = -1
-
+    stride = 4 * cap + SUB
+
+    @pl.loop(0, devices)
+    def _(d):
+        tags = pl.multiple_of(d * stride + 4 * cap, SUB)
+        send[pl.ds(tags, SUB), :] = jnp.full((SUB, LANES), -1.0, F32)
+
+    lane = lax.broadcasted_iota(I32, (1, LANES), 1)
     cell = lax.broadcasted_iota(I32, (LANES, LANES), 0)
 
     @pl.loop(0, wgt.shape[0] // SUB)
@@ -72,10 +76,11 @@
             o = owner[base + j]
             r = cnt[o]
             cnt[o] = r + 1
-            send_brick[o * cap + r] = brick[base + j]
+            tags = pl.ds(o * stride + 4 * cap, 1)
+            send[tags, :] = jnp.where(lane == r, brick[base + j].astype(F32), send[tags, :])
             slot[base + j] = o * (3 * cap) + r
             for c in range(4):
-                send[pl.ds(o * (4 * cap) + c * cap + r, 1), :] = sums[c : c + 1]
+                send[pl.ds(o * stride + c * cap + r, 1), :] = sums[c : c + 1]
 
 
 def grid_kernel(devices, cap, arrived, brick, count, code, g_out, r_out, d_out, ex, ey, tot, prev, uy):
@@ -101,7 +106,7 @@
             def _(s):
                 b = brick[d * cap + s]
                 for c in range(4):
-                    tot[c, pl.ds(b, 1), :] += arrived[pl.ds(d * (4 * cap) + c * cap + s, 1), :]
+                    tot[c, pl.ds(b, 1), :] += arrived[pl.ds(d * (4 * cap + SUB) + c * cap + s, 1), :]
 
     lane = lax.broadcasted_iota(I32, (chunk, SUB, LANES), 2)
 
@@ -276,25 +281,24 @@
     def _(x):
         def body(x, y):
             strips, inner = pl.ds(y, chunk), pl.ds(y + 1, chunk)
+            rows = pl.ds(pl.multiple_of((x * span_y + y) * SUB, SUB), chunk * SUB)
             p = p3[x + 1, inner]
             after = (p3[x + 2, inner], p3[x + 1, pl.ds(y + 2, chunk)], onward(p))
             link = (rx[x + 1, strips], ry[x, inner], rz[x, strips])
             for a in range(3):
-                shut = jnp.where(link[a] > 0.0, 0.0, -g[a, x, strips])
-                g[a, x, strips] = shut + link[a] * (p - after[a])
+                shut = jnp.where(link[a] > 0.0, 0.0, -g[a, rows, :].reshape(chunk, SUB, LANES))
+                change = shut + link[a] * (p - after[a])
+                g[a, rows, :] = change.reshape(chunk * SUB, LANES)
 
         layer(x, body)
-
-    per_layer = span_y * SUB
 
     @pl.loop(0, devices)
     def _(d):
-        @pl.loop(0, cap)
+        @pl.loop(0, cap, unroll=8)
         def _(s):
             b = jnp.maximum(brick[d * cap + s], 0)
             for a in range(3):
-                row = g[a, b // per_layer, (b // SUB) % span_y, pl.ds(b % SUB, 1), :]
-                reply[d * 3 + a, pl.ds(s, 1), :] = row
+                reply[pl.ds(d * (3 * cap) + a * cap + s, 1), :] = g[a, pl.ds(b, 1), :]
 
     leave.wait()
 
@@ -355,15 +359,15 @@
     wall_x = shifted(open_cell[:1], "slab", -1)
     wall_y = shifted(open_cell[:, :1], "sub", -1)
 
-    send, send_brick, slot = pl.pallas_call(
+    stride = 4 * cap + SUB
+    send, slot = pl.pallas_call(
         functools.partial(splat_kernel, devices, cap),
         out_shape=(
-            struct((devices * 4 * cap, LANES)),
-            struct((devices * cap,), I32),
+            struct((devices * stride, LANES)),
             struct((blocks,), I32),
         ),
         in_specs=[vmem(), vmem(), vmem(), smem(), smem()],
-        out_specs=(vmem(), smem(), smem()),
+        out_specs=(vmem(), smem()),
         scratch_shapes=[pltpu.SMEM((devices,), I32), pltpu.VMEM((8 * SUB, LANES), F32)],
         compiler_params=params(),
         name="splat",
@@ -372,8 +376,8 @@
     exchange = functools.partial(
         lax.all_to_all, axis_name=("slab", "sub"), split_axis=0, concat_axis=0, tiled=True
     )
-    arrived_brick = exchange(send_brick.reshape(devices, cap))
-    arrived = exchange(send.reshape(devices, 4 * cap, LANES))
+    arrived = exchange(send.reshape(devices, stride, LANES))
+    arrived_brick = arrived[:, 4 * cap, :cap].astype(I32)
     count = jnp.sum((arrived_brick >= 0).astype(I32), axis=1)
     arrived_brick = arrived_brick.reshape(devices * cap)
 
@@ -401,7 +405,7 @@
             struct((span_y, SUB, LANES)),
             struct((span_x, 1, SUB, LANES)),
         ),
-        in_specs=[whole(devices * 4 * cap, LANES), smem(), smem(), one_layer],
+        in_specs=[whole(devices * stride, LANES), smem(), smem(), one_layer],
         out_specs=(
             three,
             three,
@@ -416,12 +420,12 @@
         ],
         compiler_params=params(dimension_semantics=("arbitrary",)),
         name="grid",
-    )(arrived.reshape(devices * 4 * cap, LANES), arrived_brick, count, code)
+    )(arrived.reshape(devices * stride, LANES), arrived_brick, count, code)
 
     padded = (span_x + 2, span_y + 2, SUB, LANES)
     p, reply = pl.pallas_call(
         functools.partial(solve_kernel, devices, cap),
-        out_shape=(struct(padded), struct((devices * 3, cap, LANES))),
+        out_shape=(struct(padded), struct((devices * 3 * cap, LANES))),
         in_specs=[anywhere()] * 6 + [smem()],
         out_specs=(anywhere(), vmem()),
         scratch_shapes=[
@@ -430,7 +434,7 @@
             pltpu.VMEM(grid4, F32),
             pltpu.VMEM(grid4, F32),
             pltpu.VMEM(grid4, I32),
-            pltpu.VMEM((3,) + grid4, F32),
+            pltpu.VMEM((3, bricks, LANES), F32),
             pltpu.VMEM((span_y, SUB, LANES), F32),
             pltpu.VMEM((span_x, SUB, LANES), F32),
             pltpu.VMEM(padded, F32),
@@ -443,7 +447,7 @@
         ],
         compiler_params=params(collective_id=0, has_side_effects=True),
         name="solve",
-    )(g, r, div, code, edge_x, edge_y, arrived_brick)
+    )(g.reshape(3, bricks, LANES), r, div, code, edge_x, edge_y, arrived_brick)
 
     returned = exchange(reply.reshape(devices, 3 * cap, LANES))
 

time: 278 us -> 248 us (0.89)
  Pallas kernels: 172 us -> 153 us
  blocking collectives: 14.3 us -> 0 us
  waiting for transfers between devices: 60.8 us -> 67.8 us
  local copies, waits for them, and re-layouts: 8.25 us -> 4.62 us
    all_to_all x1 -> x0, blocking collectives: 14.3 us -> none  [on_device(): arrived_brick = exchange(send_brick.reshape(devices, cap))]
    pallas_call x1, Pallas kernels: 101 us -> 88.2 us  [on_device(): pl.pallas_call(functools.partial(solve_kernel, devices, cap), out_shape=(...]
    pallas_call x1, Pallas kernels: 25.6 us -> 19.5 us  [on_device(): pl.pallas_call(functools.partial(splat_kernel, devices, cap), out_shape=(...]
    ppermute x2, waiting for transfers between devices: 13.7 us -> 17.9 us  [shifted(): return lax.ppermute(block, axis, route)]
    all_to_all x1, starting transfers between devices: 11.8 us -> 8.06 us  [on_device(): returned = exchange(reply.reshape(devices, 3 * cap, LANES))]
    all_to_all x1, starting transfers between devices: 3.61 us -> 7.33 us  [on_device(): arrived = exchange(send.reshape(devices, stride, LANES))]
    all_to_all x1, waiting for transfers between devices: 22.5 us -> 25.4 us  [on_device(): arrived = exchange(send.reshape(devices, stride, LANES))]
  transfers between devices with their start and end apart: 4 -> 4, of which waited for: 3 -> 4; matrix products, arithmetic and copies ran while one was open for 4% -> 2% of each run, Pallas kernels for 5% -> 5%
where the time goes in v1:
time: 248 us
  Pallas kernels  153 us (62%)
  waiting for transfers between devices  67.8 us (27%)
  starting transfers between devices  18.1 us (7%)
  local copies, waits for them, and re-layouts  4.62 us (2%)
  other arithmetic  4.54 us (2%)
    pallas_call x1, Pallas kernels, on_device(): pl.pallas_call(functools.partial(solve_kernel, devices, cap), out_shape=(...  88.2 us
    all_to_all x1, waiting for transfers between devices, on_device(): arrived = exchange(send.reshape(devices, stride, LANES))  25.4 us
    all_to_all x1, waiting for transfers between devices, on_device(): returned = exchange(reply.reshape(devices, 3 * cap, LANES))  24.6 us
    pallas_call x1, Pallas kernels, on_device(): pl.pallas_call(functools.partial(grid_kernel, devices, cap), grid=(span_x...  23.3 us
    pallas_call x1, Pallas kernels, on_device(): pl.pallas_call(functools.partial(splat_kernel, devices, cap), out_shape=(...  19.5 us
    ppermute x2, waiting for transfers between devices, shifted(): return lax.ppermute(block, axis, route)  17.9 us
    pallas_call x1, Pallas kernels, on_device(): pl.pallas_call(face_kernel, grid=(span_x,), out_shape=(struct((3,) + flag...  13.1 us
    pallas_call x1, Pallas kernels, on_device(): pl.pallas_call(functools.partial(gather_kernel, cap), out_shape=struct((3...  8.39 us
  transfers between devices with their start and end apart: 4, of which 4 were waited for; matrix products, arithmetic and copies ran while one was open for 2% of the time, Pallas kernels for 5%

profile of v1, /device:TPU:0, one launch (start us, length us, event | category | flops | bytes accessed | tf_op | source)
XLA Modules:
  0.0 248.4 jit_solution(164698137843808886)
XLA Ops:
  0.6 19.5 %splat.1 = (f32[4352,128]{1,0:T(8,128)}, s32[512]{0:T(512)}) custom-call(f32[3,512,128]{2,1,0:T(8,128)} %bitcast.19, f32[512,128]{1,0:T(8,128)} %wgt.1, s32[512,128]{1,0:T(8,128)} %off.3, s32[512]{0:T(512)} %bitcast.24, s32[512]{0:T(512)} %bitcast.25), custom_call_target="tpu_custom_call" | custom-call | tf_op jit(solution)/shard_map/splat/pallas_call | solution.py:363
  20.1 7.3 %all-to-all-start = ((f32[32,136,128]{2,1,0:T(8,128)}), f32[32,136,128]{2,1,0:T(8,128)S(1)}, u32[]{:S(2)}, u32[]{:S(2)}) async-start(f32[32,136,128]{2,1,0:T(8,128)} %bitcast.21), calls=%async_computation | async-start | bytes 4456448 | tf_op jit(solution)/shard_map/all_to_all | solution.py:379
  27.5 2.0 fusion.2
  29.5 0.0 copy-start.1
  29.5 1.4 collective-permute-start
  31.0 1.3 collective-permute-start.1
  32.3 0.3 slice.27
  32.7 0.6 slice.29
  33.3 0.8 collective-permute-done.1
  34.1 17.1 %collective-permute-done = f32[1,64,1024]{2,1,0:T(8,128)S(1)} collective-permute-done((f32[1,64,1024]{2,1,0:T(8,128)S(1)}, f32[1,64,1024]{2,1,0:T(8,128)S(1)}, u32[]{:S(2)}, u32[]{:S(2)}) %collective-permute-start) | collective-permute-done | bytes 262176 | tf_op jit(solution)/shard_map/ppermute | solution.py:40
  51.3 0.0 copy-done.1
  51.3 1.2 select_add_fusion
  52.5 1.8 copy.9
  54.2 25.4 %all-to-all-done = f32[32,136,128]{2,1,0:T(8,128)S(1)} async-done(((f32[32,136,128]{2,1,0:T(8,128)}), f32[32,136,128]{2,1,0:T(8,128)S(1)}, u32[]{:S(2)}, u32[]{:S(2)}) %all-to-all-start) | async-done | bytes 2228256 | tf_op jit(solution)/shard_map/all_to_all | solution.py:379
  79.6 1.3 fusion
  80.9 0.7 convert_element_type.22.brick
  81.6 0.0 copy-done
  81.6 23.3 %grid.1 = (f32[3,8,64,8,128]{4,3,2,1,0:T(8,128)}, f32[3,8,64,8,128]{4,3,2,1,0:T(8,128)}, f32[8,64,8,128]{3,2,1,0:T(8,128)}, f32[64,8,128]{2,1,0:T(8,128)}, f32[8,1,8,128]{3,2,1,0:T(8,128)}) custom-call(f32[4352,128]{1,0:T(8,128)} %bitcast.16, s32[1024]{0:T(1024)} %convert_element_type.22.brick, s32[32]{0:T(128)} %get-tuple-element.25.count, ...), custom_call_target="tpu_custom_call" | custom-call | tf_op jit(solution)/shard_map/grid/pallas_call | solution.py:398
  104.9 88.2 %solve.1 = (f32[10,66,8,128]{3,2,1,0:T(8,128)}, f32[3072,128]{1,0:T(8,128)}) custom-call(f32[3,4096,128]{2,1,0:T(8,128)} %bitcast.13, f32[3,8,64,8,128]{4,3,2,1,0:T(8,128)} %get-tuple-element.17.r_hbm.r, f32[8,64,8,128]{3,2,1,0:T(8,128)} %get-tuple-element.18.d_hbm, s32[8,64,8,128]{3,2,1,0:T(8,128)} %bitcast.15, f32[64,8,128]{2,1,0:T(8,128)} %get-tuple-element.19.ex_hbm, ...), custom_call_target="tpu_custom_call" | custom-call | tf_op jit(solution)/shard_map/solve/pallas_call | solution.py:426
  193.1 8.1 %all-to-all-start.1 = ((f32[32,96,128]{2,1,0:T(8,128)}), f32[32,96,128]{2,1,0:T(8,128)S(1)}, u32[]{:S(2)}, u32[]{:S(2)}) async-start(f32[32,96,128]{2,1,0:T(8,128)} %bitcast.22), calls=%async_computation.1 | async-start | bytes 3145728 | tf_op jit(solution)/shard_map/all_to_all | solution.py:452
  201.2 13.1 %faces.1 = (f32[3,8,64,1024]{3,2,1,0:T(8,128)}, f32[8,64,1024]{2,1,0:T(8,128)}) custom-call(f32[3,8,64,8,128]{4,3,2,1,0:T(8,128)} %get-tuple-element.16.g, f32[3,8,64,8,128]{4,3,2,1,0:T(8,128)} %get-tuple-element.17.r_hbm.r, f32[10,66,8,128]{3,2,1,0:T(8,128)} %get-tuple-element.22.p_here.p_next, f32[10,66,8,128]{3,2,1,0:T(8,128)} %get-tuple-element.22.p_here.p_next), custom_call_target="tpu_custom_call" | custom-call | flops 10000000 | bytes 24000000 | tf_op jit(solution)/shard_map/faces/pallas_call | solution.py:454
  214.3 24.6 %all-to-all-done.1 = f32[32,96,128]{2,1,0:T(8,128)S(1)} async-done(((f32[32,96,128]{2,1,0:T(8,128)}), f32[32,96,128]{2,1,0:T(8,128)S(1)}, u32[]{:S(2)}, u32[]{:S(2)}) %all-to-all-start.1) | async-done | bytes 1572896 | tf_op jit(solution)/shard_map/all_to_all | solution.py:452
  238.9 1.1 copy-done.2
  240.0 8.4 %gather.1 = f32[3,512,128]{2,1,0:T(8,128)} custom-call(f32[3,512,128]{2,1,0:T(8,128)} %bitcast.20, s32[512,128]{1,0:T(8,128)} %off.3, s32[512]{0:T(512)} %get-tuple-element.14.slot, f32[3072,128]{1,0:T(8,128)} %bitcast.18), custom_call_target="tpu_custom_call" | custom-call | tf_op jit(solution)/shard_map/gather/pallas_call | solution.py:474
  (7 shorter events, 0.2 us)
Async XLA Ops:
  20.1 59.5 %all-to-all-start = ((f32[32,136,128]{2,1,0:T(8,128)}), f32[32,136,128]{2,1,0:T(8,128)S(1)}, u32[]{:S(2)}, u32[]{:S(2)}) async-start(f32[32,136,128]{2,1,0:T(8,128)} %bitcast.21), calls=%async_computation | async-start | bytes 4456448 | tf_op jit(solution)/shard_map/all_to_all | solution.py:379
  29.5 21.8 %copy-start.1 = (s32[8,64,1024]{2,1,0:T(8,128)S(1)}, s32[8,64,1024]{2,1,0:T(8,128)}, u32[]{:S(2)}) copy-start(s32[8,64,1024]{2,1,0:T(8,128)} %param.11) | copy-start | bytes 6291460
  29.5 21.7 %collective-permute-start = (f32[1,64,1024]{2,1,0:T(8,128)S(1)}, f32[1,64,1024]{2,1,0:T(8,128)S(1)}, u32[]{:S(2)}, u32[]{:S(2)}) collective-permute-start(f32[1,64,1024]{2,1,0:T(8,128)S(1)} %slice.26), channel_id=1, source_target_pairs={{4,0},{8,4},{12,8},{16,12},{20,16},{24,20},{28,24},{5,1},{9,5},{13... | collective-permute-start | bytes 786440 | tf_op jit(solution)/shard_map/ppermute | solution.py:40
  31.0 3.1 %collective-permute-start.1 = (f32[8,1,1024]{2,1,0:T(1,128)S(1)}, f32[8,1,1024]{2,1,0:T(1,128)S(1)}, u32[]{:S(2)}, u32[]{:S(2)}) collective-permute-start(f32[8,1,1024]{2,1,0:T(1,128)S(1)} %slice.28), channel_id=1, source_target_pairs={{1,0},{2,1},{3,2},{5,4},{6,5},{7,6},{9,8},{10,9},{11,10},{13,12},{... | collective-permute-start | bytes 98312 | tf_op jit(solution)/shard_map/ppermute | solution.py:40
  79.6 2.0 copy-start
  193.1 45.7 %all-to-all-start.1 = ((f32[32,96,128]{2,1,0:T(8,128)}), f32[32,96,128]{2,1,0:T(8,128)S(1)}, u32[]{:S(2)}, u32[]{:S(2)}) async-start(f32[32,96,128]{2,1,0:T(8,128)} %bitcast.22), calls=%async_computation.1 | async-start | bytes 3145728 | tf_op jit(solution)/shard_map/all_to_all | solution.py:452
  238.8 1.1 copy-start.2

commit v2 on v1

--- a/solution.py
+++ b/solution.py
@@ -168,34 +168,73 @@
         pl.semaphore_signal(barrier, inc=1, device_id={axis: peer}, device_id_type=MESH)
     pl.semaphore_wait(barrier, 4)
 
-    def remote(index, src, dst, axis, peer):
-        return pltpu.make_async_remote_copy(
+    def remote(index, src, dst, axis, up):
+        place, size = (slab, n_slab) if axis == "slab" else (sub, n_sub)
+        after, before = place < size - 1, place > 0
+        peer = {"slab": (east, west), "sub": (north, south)}[axis][0 if up else 1]
+        copy = pltpu.make_async_remote_copy(
             src_ref=src, dst_ref=dst, send_sem=send_sem.at[index], recv_sem=recv_sem.at[index],
             device_id={axis: peer}, device_id_type=MESH,
         )
-
-    edges = [
-        remote(0, ex_hbm, hx, "slab", east),
-        remote(1, ey_hbm.at[:, 0], hy, "sub", north),
-        remote(2, r_hbm.at[0, span_x - 1], rx.at[0], "slab", east),
-        remote(3, r_hbm.at[1, :, span_y - 1], ry.at[:, 0], "sub", north),
-    ]
-    for copy in edges:
-        copy.start()
+        return copy, (after if up else before), (before if up else after)
+
+    def begin(*moves):
+        for copy, sends, _ in moves:
+            pl.when(sends)(copy.start)
+
+    def finish(*moves):
+        for copy, sends, gets in moves:
+            pl.when(sends)(copy.wait_send)
+            pl.when(gets)(copy.wait_recv)
 
     xs, ys = pl.ds(1, span_x), pl.ds(1, span_y)
-
-    def x_halo(field, first, both):
-        copies = [remote(first, field.at[1, ys], field.at[span_x + 1, ys], "slab", west)]
-        if both:
-            copies.append(remote(first + 1, field.at[span_x, ys], field.at[0, ys], "slab", east))
-        return copies
-
-    def y_halo(field, first, both):
-        copies = [remote(first, field.at[xs, 1], field.at[xs, span_y + 1], "sub", south)]
-        if both:
-            copies.append(remote(first + 1, field.at[xs, span_y], field.at[xs, 0], "sub", north))
-        return copies
+    flow_x = remote(0, ex_hbm, hx, "slab", True)
+    flow_y = remote(1, ey_hbm.at[:, 0], hy, "sub", True)
+    link_x = remote(2, r_hbm.at[0, span_x - 1], rx.at[0], "slab", True)
+    link_y = remote(3, r_hbm.at[1, :, span_y - 1], ry.at[:, 0], "sub", True)
+    begin(flow_y, flow_x)
+
+    def halos(field, first):
+        return (
+            remote(first, field.at[1, ys], field.at[span_x + 1, ys], "slab", False),
+            remote(first + 1, field.at[span_x, ys], field.at[0, ys], "slab", True),
+            remote(first + 2, field.at[xs, 1], field.at[xs, span_y + 1], "sub", False),
+            remote(first + 3, field.at[xs, span_y], field.at[xs, 0], "sub", True),
+        )
+
+    nothing = jnp.zeros((SUB, LANES), F32)
+
+    @pl.when(slab == 0)
+    def _():
+        @pl.loop(0, span_y)
+        def _(y):
+            hx[y] = nothing
+            rx[0, y] = nothing
+            for field in (p1, p2):
+                field[0, y + 1] = nothing
+
+    @pl.when(slab == n_slab - 1)
+    def _():
+        @pl.loop(0, span_y)
+        def _(y):
+            for field in (p1, p2, p3):
+                field[span_x + 1, y + 1] = nothing
+
+    @pl.when(sub == 0)
+    def _():
+        @pl.loop(0, span_x)
+        def _(x):
+            hy[x] = nothing
+            ry[x, 0] = nothing
+            for field in (p1, p2):
+                field[x + 1, 0] = nothing
+
+    @pl.when(sub == n_sub - 1)
+    def _():
+        @pl.loop(0, span_x)
+        def _(x):
+            for field in (p1, p2, p3):
+                field[x + 1, span_y + 1] = nothing
 
     lane = lax.broadcasted_iota(I32, (chunk, SUB, LANES), 2)
 
@@ -207,53 +246,40 @@
         turned = pltpu.roll(value, 1, 2)
         return jnp.where(lane == 0, pltpu.roll(turned, 1, 1), turned)
 
-    def layer(x, body):
-        @pl.loop(0, span_y // chunk)
-        def _(k):
-            body(x, k * chunk)
-
-    def sweep(field, body, first, both):
-        layer(0, body)
-        layer(span_x - 1, body)
-        copies = x_halo(field, first, both)
-        for copy in copies:
-            copy.start()
-
-        @pl.loop(1, span_x - 1)
+    def layers(low, high, body):
+        @pl.loop(low, high)
         def _(x):
-            layer(x, body)
-
-        later = y_halo(field, first + 2, both)
-        for copy in later:
-            copy.start()
-        for copy in copies + later:
-            copy.wait()
+            @pl.loop(0, span_y // chunk)
+            def _(k):
+                body(x, k * chunk)
 
     def lifted(x, y, raised):
         wet = kind[x, pl.ds(y, chunk)] >= 8
         return jnp.where(wet, jnp.maximum(raised, 0.0), 0.0)
 
+    def start(x, y):
+        p1[x + 1, pl.ds(y + 1, chunk)] = lifted(x, y, -step_size * div[x, pl.ds(y, chunk)])
+
     for i in (0, 1):
         locals_[i].wait()
-    for copy in edges:
-        copy.wait()
-    first_x = (slab > 0).astype(F32)
-    first_y = (sub > 0).astype(F32)
+    finish(flow_y)
+
+    @pl.loop(0, span_x)
+    def _(x):
+        div[x, 0] = div[x, 0] - hy[x]
+
+    down, up, south_1, north_1 = halos(p1, 4)
+    layers(span_x - 1, span_x, start)
+    begin(up, link_x, link_y)
+    layers(1, span_x - 1, start)
+    finish(flow_x)
 
     @pl.loop(0, span_y)
     def _(y):
-        div[0, y] = div[0, y] - first_x * hx[y]
-        rx[0, y] = first_x * rx[0, y]
-
-    @pl.loop(0, span_x)
-    def _(x):
-        div[x, 0] = div[x, 0] - first_y * hy[x]
-        ry[x, 0] = first_y * ry[x, 0]
-
-    def start(x, y):
-        p1[x + 1, pl.ds(y + 1, chunk)] = lifted(x, y, -step_size * div[x, pl.ds(y, chunk)])
-
-    sweep(p1, start, 4, True)
+        div[0, y] = div[0, y] - hx[y]
+
+    layers(0, 1, start)
+    begin(down, south_1, north_1)
     for i in (2, 3, 4):
         locals_[i].wait()
 
@@ -271,26 +297,44 @@
 
         return body
 
-    sweep(p2, ascend(p1, p2), 8, True)
-    sweep(p3, ascend(p2, p3), 12, False)
+    body = ascend(p1, p2)
+    down_2, up_2, south_2, north_2 = halos(p2, 8)
+    finish(link_y, south_1, north_1)
+    layers(1, span_x - 1, body)
+    finish(link_x, up, down)
+    layers(0, 1, body)
+    begin(down_2)
+    layers(span_x - 1, span_x, body)
+    begin(up_2, south_2, north_2)
+
+    body = ascend(p2, p3)
+    down_3, _, south_3, _ = halos(p3, 12)
+    finish(south_2, north_2)
+    layers(1, span_x - 1, body)
+    finish(up_2, down_2)
+    layers(0, 1, body)
+    begin(down_3)
+    layers(span_x - 1, span_x, body)
+    begin(south_3)
     locals_[5].wait()
+
+    def settle(x, y):
+        strips, inner = pl.ds(y, chunk), pl.ds(y + 1, chunk)
+        rows = pl.ds(pl.multiple_of((x * span_y + y) * SUB, SUB), chunk * SUB)
+        p = p3[x + 1, inner]
+        after = (p3[x + 2, inner], p3[x + 1, pl.ds(y + 2, chunk)], onward(p))
+        link = (rx[x + 1, strips], ry[x, inner], rz[x, strips])
+        for a in range(3):
+            shut = jnp.where(link[a] > 0.0, 0.0, -g[a, rows, :].reshape(chunk, SUB, LANES))
+            change = shut + link[a] * (p - after[a])
+            g[a, rows, :] = change.reshape(chunk * SUB, LANES)
+
+    finish(south_3)
+    layers(0, span_x - 1, settle)
+    finish(down_3)
     leave = pltpu.make_async_copy(p3, p_out, out_sem)
     leave.start()
-
-    @pl.loop(0, span_x)
-    def _(x):
-        def body(x, y):
-            strips, inner = pl.ds(y, chunk), pl.ds(y + 1, chunk)
-            rows = pl.ds(pl.multiple_of((x * span_y + y) * SUB, SUB), chunk * SUB)
-            p = p3[x + 1, inner]
-            after = (p3[x + 2, inner], p3[x + 1, pl.ds(y + 2, chunk)], onward(p))
-            link = (rx[x + 1, strips], ry[x, inner], rz[x, strips])
-            for a in range(3):
-                shut = jnp.where(link[a] > 0.0, 0.0, -g[a, rows, :].reshape(chunk, SUB, LANES))
-                change = shut + link[a] * (p - after[a])
-                g[a, rows, :] = change.reshape(chunk * SUB, LANES)
-
-        layer(x, body)
+    layers(span_x - 1, span_x, settle)
 
     @pl.loop(0, devices)
     def _(d):

time: 248 us -> 238 us (0.960)
  Pallas kernels: 153 us -> 134 us
  starting transfers between devices: 18.1 us -> 26.7 us
    pallas_call x1, Pallas kernels: 88.2 us -> 74.6 us  [on_device(): pl.pallas_call(functools.partial(solve_kernel, devices, cap), out_shape=(...]
    all_to_all x1, starting transfers between devices: 8.06 us -> 16.7 us  [on_device(): returned = exchange(reply.reshape(devices, 3 * cap, LANES))]
    pallas_call x1, Pallas kernels: 23.3 us -> 18.2 us  [on_device(): pl.pallas_call(functools.partial(grid_kernel, devices, cap), grid=(span_x...]
  transfers between devices with their start and end apart: 4 -> 4, of which waited for: 4 -> 4; matrix products, arithmetic and copies ran while one was open for 2% -> 3% of each run, Pallas kernels for 5% -> 5%
where the time goes in v2:
time: 238 us
  Pallas kernels  134 us (56%)
  waiting for transfers between devices  67.8 us (28%)
  starting transfers between devices  26.7 us (11%)
  local copies, waits for them, and re-layouts  4.62 us (2%)
  other arithmetic  4.54 us (2%)
    pallas_call x1, Pallas kernels, on_device(): pl.pallas_call(functools.partial(solve_kernel, devices, cap), out_shape=(...  74.6 us
    all_to_all x1, waiting for transfers between devices, on_device(): arrived = exchange(send.reshape(devices, stride, LANES))  25.4 us
    all_to_all x1, waiting for transfers between devices, on_device(): returned = exchange(reply.reshape(devices, 3 * cap, LANES))  24.6 us
    pallas_call x1, Pallas kernels, on_device(): pl.pallas_call(functools.partial(splat_kernel, devices, cap), out_shape=(...  19.5 us
    pallas_call x1, Pallas kernels, on_device(): pl.pallas_call(functools.partial(grid_kernel, devices, cap), grid=(span_x...  18.2 us
    ppermute x2, waiting for transfers between devices, shifted(): return lax.ppermute(block, axis, route)  17.9 us
    all_to_all x1, starting transfers between devices, on_device(): returned = exchange(reply.reshape(devices, 3 * cap, LANES))  16.7 us
    pallas_call x1, Pallas kernels, on_device(): pl.pallas_call(face_kernel, grid=(span_x,), out_shape=(struct((3,) + flag...  13.1 us
  transfers between devices with their start and end apart: 4, of which 4 were waited for; matrix products, arithmetic and copies ran while one was open for 3% of the time, Pallas kernels for 5%

profile of v2, /device:TPU:0, one launch (start us, length us, event | category | flops | bytes accessed | tf_op | source)
XLA Modules:
  0.0 238.3 jit_solution(14025367105131076022)
XLA Ops:
  0.6 19.5 %splat.1 = (f32[4352,128]{1,0:T(8,128)}, s32[512]{0:T(512)}) custom-call(f32[3,512,128]{2,1,0:T(8,128)} %bitcast.19, f32[512,128]{1,0:T(8,128)} %wgt.1, s32[512,128]{1,0:T(8,128)} %off.3, s32[512]{0:T(512)} %bitcast.24, s32[512]{0:T(512)} %bitcast.25), custom_call_target="tpu_custom_call" | custom-call | tf_op jit(solution)/shard_map/splat/pallas_call | solution.py:407
  20.1 7.3 %all-to-all-start = ((f32[32,136,128]{2,1,0:T(8,128)}), f32[32,136,128]{2,1,0:T(8,128)S(1)}, u32[]{:S(2)}, u32[]{:S(2)}) async-start(f32[32,136,128]{2,1,0:T(8,128)} %bitcast.21), calls=%async_computation | async-start | bytes 4456448 | tf_op jit(solution)/shard_map/all_to_all | solution.py:423
  27.5 2.0 fusion.2
  29.5 0.0 copy-start.1
  29.5 1.4 collective-permute-start
  31.0 1.3 collective-permute-start.1
  32.3 0.3 slice.27
  32.7 0.6 slice.29
  33.3 0.8 collective-permute-done.1
  34.1 17.1 %collective-permute-done = f32[1,64,1024]{2,1,0:T(8,128)S(1)} collective-permute-done((f32[1,64,1024]{2,1,0:T(8,128)S(1)}, f32[1,64,1024]{2,1,0:T(8,128)S(1)}, u32[]{:S(2)}, u32[]{:S(2)}) %collective-permute-start) | collective-permute-done | bytes 262176 | tf_op jit(solution)/shard_map/ppermute | solution.py:40
  51.3 0.0 copy-done.1
  51.3 1.2 select_add_fusion
  52.5 1.8 copy.9
  54.2 25.4 %all-to-all-done = f32[32,136,128]{2,1,0:T(8,128)S(1)} async-done(((f32[32,136,128]{2,1,0:T(8,128)}), f32[32,136,128]{2,1,0:T(8,128)S(1)}, u32[]{:S(2)}, u32[]{:S(2)}) %all-to-all-start) | async-done | bytes 2228256 | tf_op jit(solution)/shard_map/all_to_all | solution.py:423
  79.6 1.3 fusion
  80.9 0.7 convert_element_type.22.brick
  81.6 0.0 copy-done
  81.6 18.2 %grid.1 = (f32[3,8,64,8,128]{4,3,2,1,0:T(8,128)}, f32[3,8,64,8,128]{4,3,2,1,0:T(8,128)}, f32[8,64,8,128]{3,2,1,0:T(8,128)}, f32[64,8,128]{2,1,0:T(8,128)}, f32[8,1,8,128]{3,2,1,0:T(8,128)}) custom-call(f32[4352,128]{1,0:T(8,128)} %bitcast.16, s32[1024]{0:T(1024)} %convert_element_type.22.brick, s32[32]{0:T(128)} %get-tuple-element.25.count, ...), custom_call_target="tpu_custom_call" | custom-call | tf_op jit(solution)/shard_map/grid/pallas_call | solution.py:442
  99.8 74.6 %solve.1 = (f32[10,66,8,128]{3,2,1,0:T(8,128)}, f32[3072,128]{1,0:T(8,128)}) custom-call(f32[3,4096,128]{2,1,0:T(8,128)} %bitcast.13, f32[3,8,64,8,128]{4,3,2,1,0:T(8,128)} %get-tuple-element.17.r_hbm.r, f32[8,64,8,128]{3,2,1,0:T(8,128)} %get-tuple-element.18.d_hbm, s32[8,64,8,128]{3,2,1,0:T(8,128)} %bitcast.15, f32[64,8,128]{2,1,0:T(8,128)} %get-tuple-element.19.ex_hbm, ...), custom_call_target="tpu_custom_call" | custom-call | tf_op jit(solution)/shard_map/solve/pallas_call | solution.py:470
  174.5 16.7 %all-to-all-start.1 = ((f32[32,96,128]{2,1,0:T(8,128)}), f32[32,96,128]{2,1,0:T(8,128)S(1)}, u32[]{:S(2)}, u32[]{:S(2)}) async-start(f32[32,96,128]{2,1,0:T(8,128)} %bitcast.22), calls=%async_computation.1 | async-start | bytes 3145728 | tf_op jit(solution)/shard_map/all_to_all | solution.py:496
  191.2 13.1 %faces.1 = (f32[3,8,64,1024]{3,2,1,0:T(8,128)}, f32[8,64,1024]{2,1,0:T(8,128)}) custom-call(f32[3,8,64,8,128]{4,3,2,1,0:T(8,128)} %get-tuple-element.16.g, f32[3,8,64,8,128]{4,3,2,1,0:T(8,128)} %get-tuple-element.17.r_hbm.r, f32[10,66,8,128]{3,2,1,0:T(8,128)} %get-tuple-element.22.p_here.p_next, f32[10,66,8,128]{3,2,1,0:T(8,128)} %get-tuple-element.22.p_here.p_next), custom_call_target="tpu_custom_call" | custom-call | flops 10000000 | bytes 24000000 | tf_op jit(solution)/shard_map/faces/pallas_call | solution.py:498
  204.2 24.6 %all-to-all-done.1 = f32[32,96,128]{2,1,0:T(8,128)S(1)} async-done(((f32[32,96,128]{2,1,0:T(8,128)}), f32[32,96,128]{2,1,0:T(8,128)S(1)}, u32[]{:S(2)}, u32[]{:S(2)}) %all-to-all-start.1) | async-done | bytes 1572896 | tf_op jit(solution)/shard_map/all_to_all | solution.py:496
  228.8 1.1 copy-done.2
  229.9 8.4 %gather.1 = f32[3,512,128]{2,1,0:T(8,128)} custom-call(f32[3,512,128]{2,1,0:T(8,128)} %bitcast.20, s32[512,128]{1,0:T(8,128)} %off.3, s32[512]{0:T(512)} %get-tuple-element.14.slot, f32[3072,128]{1,0:T(8,128)} %bitcast.18), custom_call_target="tpu_custom_call" | custom-call | tf_op jit(solution)/shard_map/gather/pallas_call | solution.py:518
  (7 shorter events, 0.2 us)
Async XLA Ops:
  20.1 59.5 %all-to-all-start = ((f32[32,136,128]{2,1,0:T(8,128)}), f32[32,136,128]{2,1,0:T(8,128)S(1)}, u32[]{:S(2)}, u32[]{:S(2)}) async-start(f32[32,136,128]{2,1,0:T(8,128)} %bitcast.21), calls=%async_computation | async-start | bytes 4456448 | tf_op jit(solution)/shard_map/all_to_all | solution.py:423
  29.5 21.8 %copy-start.1 = (s32[8,64,1024]{2,1,0:T(8,128)S(1)}, s32[8,64,1024]{2,1,0:T(8,128)}, u32[]{:S(2)}) copy-start(s32[8,64,1024]{2,1,0:T(8,128)} %param.11) | copy-start | bytes 6291460
  29.5 21.7 %collective-permute-start = (f32[1,64,1024]{2,1,0:T(8,128)S(1)}, f32[1,64,1024]{2,1,0:T(8,128)S(1)}, u32[]{:S(2)}, u32[]{:S(2)}) collective-permute-start(f32[1,64,1024]{2,1,0:T(8,128)S(1)} %slice.26), channel_id=1, source_target_pairs={{4,0},{8,4},{12,8},{16,12},{20,16},{24,20},{28,24},{5,1},{9,5},{13... | collective-permute-start | bytes 786440 | tf_op jit(solution)/shard_map/ppermute | solution.py:40
  31.0 3.1 %collective-permute-start.1 = (f32[8,1,1024]{2,1,0:T(1,128)S(1)}, f32[8,1,1024]{2,1,0:T(1,128)S(1)}, u32[]{:S(2)}, u32[]{:S(2)}) collective-permute-start(f32[8,1,1024]{2,1,0:T(1,128)S(1)} %slice.28), channel_id=1, source_target_pairs={{1,0},{2,1},{3,2},{5,4},{6,5},{7,6},{9,8},{10,9},{11,10},{13,12},{... | collective-permute-start | bytes 98312 | tf_op jit(solution)/shard_map/ppermute | solution.py:40
  79.6 2.0 copy-start
  174.5 54.3 %all-to-all-start.1 = ((f32[32,96,128]{2,1,0:T(8,128)}), f32[32,96,128]{2,1,0:T(8,128)S(1)}, u32[]{:S(2)}, u32[]{:S(2)}) async-start(f32[32,96,128]{2,1,0:T(8,128)} %bitcast.22), calls=%async_computation.1 | async-start | bytes 3145728 | tf_op jit(solution)/shard_map/all_to_all | solution.py:496
  228.8 1.1 copy-start.2

commit v3 on v2

--- a/solution.py
+++ b/solution.py
@@ -86,7 +86,7 @@
 def grid_kernel(devices, cap, arrived, brick, count, code, g_out, r_out, d_out, ex, ey, tot, prev, uy):
     x = pl.program_id(0)
     span_y = code.shape[1]
-    chunk = 4
+    chunk = SUB
 
     @pl.when(x == 0)
     def _():
@@ -102,11 +102,22 @@
 
         @pl.loop(0, devices)
         def _(d):
-            @pl.loop(0, count[d])
-            def _(s):
+            used = count[d]
+
+            @pl.loop(0, lax.div(used + 1, 2))
+            def _(pair):
+                s = 2 * pair
+                second = s + 1 < used
                 b = brick[d * cap + s]
+                b_second = jnp.where(second, brick[d * cap + s + 1], b)
+                same = b_second == b
                 for c in range(4):
-                    tot[c, pl.ds(b, 1), :] += arrived[pl.ds(d * (4 * cap + SUB) + c * cap + s, 1), :]
+                    row = d * (4 * cap + SUB) + c * cap + s
+                    held = tot[c, pl.ds(b, 1), :] + arrived[pl.ds(row, 1), :]
+                    other = jnp.where(same, held, tot[c, pl.ds(b_second, 1), :])
+                    added = jnp.where(second, arrived[pl.ds(row + 1, 1), :], 0.0)
+                    tot[c, pl.ds(b, 1), :] = held
+                    tot[c, pl.ds(b_second, 1), :] = other + added
 
     lane = lax.broadcasted_iota(I32, (chunk, SUB, LANES), 2)
 
@@ -143,7 +154,7 @@
     rx, ry, rz, div, kind, g, hx, hy, p1, p2, p3, here, out_sem, send_sem, recv_sem,
 ):
     span_x, span_y = div.shape[0], div.shape[1]
-    chunk = 4
+    chunk = SUB
     n_slab, n_sub = lax.axis_size("slab"), lax.axis_size("sub")
     slab, sub = lax.axis_index("slab"), lax.axis_index("sub")
     east, west = lax.rem(slab + 1, n_slab), lax.rem(slab + n_slab - 1, n_slab)

time: 238 us -> 216 us (0.908); the launches traced: 238 us -> 219 us
  Pallas kernels: 134 us -> 114 us
    pallas_call x1, Pallas kernels: 74.6 us -> 57.4 us  [on_device(): pl.pallas_call(functools.partial(solve_kernel, devices, cap), out_shape=(...]
    pallas_call x1, Pallas kernels: 18.2 us -> 15.8 us  [on_device(): pl.pallas_call(functools.partial(grid_kernel, devices, cap), grid=(span_x...]
  transfers between devices with their start and end apart: 4 -> 4, of which waited for: 4 -> 4; matrix products, arithmetic and copies ran while one was open for 3% -> 3% of each run, Pallas kernels for 5% -> 6%
where the time goes in v3:
time: 216 us; the launch traced here: 219 us
  Pallas kernels  114 us (53%)
  waiting for transfers between devices  67.8 us (31%)
  starting transfers between devices  27.2 us (13%)
  local copies, waits for them, and re-layouts  4.62 us (2%)
  other arithmetic  4.54 us (2%)
    pallas_call x1, Pallas kernels, on_device(): pl.pallas_call(functools.partial(solve_kernel, devices, cap), out_shape=(...  57.4 us
    all_to_all x1, waiting for transfers between devices, on_device(): arrived = exchange(send.reshape(devices, stride, LANES))  25.4 us
    all_to_all x1, waiting for transfers between devices, on_device(): returned = exchange(reply.reshape(devices, 3 * cap, LANES))  24.6 us
    pallas_call x1, Pallas kernels, on_device(): pl.pallas_call(functools.partial(splat_kernel, devices, cap), out_shape=(...  19.5 us
    ppermute x2, waiting for transfers between devices, shifted(): return lax.ppermute(block, axis, route)  17.9 us
    all_to_all x1, starting transfers between devices, on_device(): returned = exchange(reply.reshape(devices, 3 * cap, LANES))  17.2 us
    pallas_call x1, Pallas kernels, on_device(): pl.pallas_call(functools.partial(grid_kernel, devices, cap), grid=(span_x...  15.8 us
    pallas_call x1, Pallas kernels, on_device(): pl.pallas_call(face_kernel, grid=(span_x,), out_shape=(struct((3,) + flag...  13.1 us
  transfers between devices with their start and end apart: 4, of which 4 were waited for; matrix products, arithmetic and copies ran while one was open for 3% of the time, Pallas kernels for 6%

profile of v3, /device:TPU:0, one launch (start us, length us, event | category | flops | bytes accessed | tf_op | source)
XLA Modules:
  0.0 219.2 jit_solution(13809058901766239848)
XLA Ops:
  0.6 19.5 %splat.1 = (f32[4352,128]{1,0:T(8,128)}, s32[512]{0:T(512)}) custom-call(f32[3,512,128]{2,1,0:T(8,128)} %bitcast.19, f32[512,128]{1,0:T(8,128)} %wgt.1, s32[512,128]{1,0:T(8,128)} %off.3, s32[512]{0:T(512)} %bitcast.24, s32[512]{0:T(512)} %bitcast.25), custom_call_target="tpu_custom_call" | custom-call | tf_op jit(solution)/shard_map/splat/pallas_call | solution.py:418
  20.1 7.3 %all-to-all-start = ((f32[32,136,128]{2,1,0:T(8,128)}), f32[32,136,128]{2,1,0:T(8,128)S(1)}, u32[]{:S(2)}, u32[]{:S(2)}) async-start(f32[32,136,128]{2,1,0:T(8,128)} %bitcast.21), calls=%async_computation | async-start | bytes 4456448 | tf_op jit(solution)/shard_map/all_to_all | solution.py:434
  27.5 2.0 fusion.2
  29.5 0.0 copy-start.1
  29.5 1.4 collective-permute-start
  31.0 1.3 collective-permute-start.1
  32.3 0.3 slice.27
  32.7 0.6 slice.29
  33.3 0.8 collective-permute-done.1
  34.1 17.1 %collective-permute-done = f32[1,64,1024]{2,1,0:T(8,128)S(1)} collective-permute-done((f32[1,64,1024]{2,1,0:T(8,128)S(1)}, f32[1,64,1024]{2,1,0:T(8,128)S(1)}, u32[]{:S(2)}, u32[]{:S(2)}) %collective-permute-start) | collective-permute-done | bytes 262176 | tf_op jit(solution)/shard_map/ppermute | solution.py:40
  51.3 0.0 copy-done.1
  51.3 1.2 select_add_fusion
  52.5 1.8 copy.9
  54.2 25.4 %all-to-all-done = f32[32,136,128]{2,1,0:T(8,128)S(1)} async-done(((f32[32,136,128]{2,1,0:T(8,128)}), f32[32,136,128]{2,1,0:T(8,128)S(1)}, u32[]{:S(2)}, u32[]{:S(2)}) %all-to-all-start) | async-done | bytes 2228256 | tf_op jit(solution)/shard_map/all_to_all | solution.py:434
  79.6 1.3 fusion
  80.9 0.7 convert_element_type.22.brick
  81.6 0.0 copy-done
  81.6 15.8 %grid.1 = (f32[3,8,64,8,128]{4,3,2,1,0:T(8,128)}, f32[3,8,64,8,128]{4,3,2,1,0:T(8,128)}, f32[8,64,8,128]{3,2,1,0:T(8,128)}, f32[64,8,128]{2,1,0:T(8,128)}, f32[8,1,8,128]{3,2,1,0:T(8,128)}) custom-call(f32[4352,128]{1,0:T(8,128)} %bitcast.16, s32[1024]{0:T(1024)} %convert_element_type.22.brick, s32[32]{0:T(128)} %get-tuple-element.25.count, ...), custom_call_target="tpu_custom_call" | custom-call | tf_op jit(solution)/shard_map/grid/pallas_call | solution.py:453
  97.4 57.4 %solve.1 = (f32[10,66,8,128]{3,2,1,0:T(8,128)}, f32[3072,128]{1,0:T(8,128)}) custom-call(f32[3,4096,128]{2,1,0:T(8,128)} %bitcast.13, f32[3,8,64,8,128]{4,3,2,1,0:T(8,128)} %get-tuple-element.17.r_hbm.r, f32[8,64,8,128]{3,2,1,0:T(8,128)} %get-tuple-element.18.d_hbm, s32[8,64,8,128]{3,2,1,0:T(8,128)} %bitcast.15, f32[64,8,128]{2,1,0:T(8,128)} %get-tuple-element.19.ex_hbm, ...), custom_call_target="tpu_custom_call" | custom-call | tf_op jit(solution)/shard_map/solve/pallas_call | solution.py:481
  154.8 17.2 %all-to-all-start.1 = ((f32[32,96,128]{2,1,0:T(8,128)}), f32[32,96,128]{2,1,0:T(8,128)S(1)}, u32[]{:S(2)}, u32[]{:S(2)}) async-start(f32[32,96,128]{2,1,0:T(8,128)} %bitcast.22), calls=%async_computation.1 | async-start | bytes 3145728 | tf_op jit(solution)/shard_map/all_to_all | solution.py:507
  172.0 13.1 %faces.1 = (f32[3,8,64,1024]{3,2,1,0:T(8,128)}, f32[8,64,1024]{2,1,0:T(8,128)}) custom-call(f32[3,8,64,8,128]{4,3,2,1,0:T(8,128)} %get-tuple-element.16.g, f32[3,8,64,8,128]{4,3,2,1,0:T(8,128)} %get-tuple-element.17.r_hbm.r, f32[10,66,8,128]{3,2,1,0:T(8,128)} %get-tuple-element.22.p_here.p_next, f32[10,66,8,128]{3,2,1,0:T(8,128)} %get-tuple-element.22.p_here.p_next), custom_call_target="tpu_custom_call" | custom-call | flops 10000000 | bytes 24000000 | tf_op jit(solution)/shard_map/faces/pallas_call | solution.py:509
  185.1 24.6 %all-to-all-done.1 = f32[32,96,128]{2,1,0:T(8,128)S(1)} async-done(((f32[32,96,128]{2,1,0:T(8,128)}), f32[32,96,128]{2,1,0:T(8,128)S(1)}, u32[]{:S(2)}, u32[]{:S(2)}) %all-to-all-start.1) | async-done | bytes 1572896 | tf_op jit(solution)/shard_map/all_to_all | solution.py:507
  209.7 1.1 copy-done.2
  210.8 8.4 %gather.1 = f32[3,512,128]{2,1,0:T(8,128)} custom-call(f32[3,512,128]{2,1,0:T(8,128)} %bitcast.20, s32[512,128]{1,0:T(8,128)} %off.3, s32[512]{0:T(512)} %get-tuple-element.14.slot, f32[3072,128]{1,0:T(8,128)} %bitcast.18), custom_call_target="tpu_custom_call" | custom-call | tf_op jit(solution)/shard_map/gather/pallas_call | solution.py:529
  (7 shorter events, 0.2 us)
Async XLA Ops:
  20.1 59.5 %all-to-all-start = ((f32[32,136,128]{2,1,0:T(8,128)}), f32[32,136,128]{2,1,0:T(8,128)S(1)}, u32[]{:S(2)}, u32[]{:S(2)}) async-start(f32[32,136,128]{2,1,0:T(8,128)} %bitcast.21), calls=%async_computation | async-start | bytes 4456448 | tf_op jit(solution)/shard_map/all_to_all | solution.py:434
  29.5 21.8 %copy-start.1 = (s32[8,64,1024]{2,1,0:T(8,128)S(1)}, s32[8,64,1024]{2,1,0:T(8,128)}, u32[]{:S(2)}) copy-start(s32[8,64,1024]{2,1,0:T(8,128)} %param.11) | copy-start | bytes 6291460
  29.5 21.7 %collective-permute-start = (f32[1,64,1024]{2,1,0:T(8,128)S(1)}, f32[1,64,1024]{2,1,0:T(8,128)S(1)}, u32[]{:S(2)}, u32[]{:S(2)}) collective-permute-start(f32[1,64,1024]{2,1,0:T(8,128)S(1)} %slice.26), channel_id=1, source_target_pairs={{4,0},{8,4},{12,8},{16,12},{20,16},{24,20},{28,24},{5,1},{9,5},{13... | collective-permute-start | bytes 786440 | tf_op jit(solution)/shard_map/ppermute | solution.py:40
  31.0 3.1 %collective-permute-start.1 = (f32[8,1,1024]{2,1,0:T(1,128)S(1)}, f32[8,1,1024]{2,1,0:T(1,128)S(1)}, u32[]{:S(2)}, u32[]{:S(2)}) collective-permute-start(f32[8,1,1024]{2,1,0:T(1,128)S(1)} %slice.28), channel_id=1, source_target_pairs={{1,0},{2,1},{3,2},{5,4},{6,5},{7,6},{9,8},{10,9},{11,10},{13,12},{... | collective-permute-start | bytes 98312 | tf_op jit(solution)/shard_map/ppermute | solution.py:40
  79.6 2.0 copy-start
  154.8 54.8 %all-to-all-start.1 = ((f32[32,96,128]{2,1,0:T(8,128)}), f32[32,96,128]{2,1,0:T(8,128)S(1)}, u32[]{:S(2)}, u32[]{:S(2)}) async-start(f32[32,96,128]{2,1,0:T(8,128)} %bitcast.22), calls=%async_computation.1 | async-start | bytes 3145728 | tf_op jit(solution)/shard_map/all_to_all | solution.py:507
  209.7 1.1 copy-start.2

commit v4 on v3

--- a/solution.py
+++ b/solution.py
@@ -55,7 +55,7 @@
     lane = lax.broadcasted_iota(I32, (1, LANES), 1)
     cell = lax.broadcasted_iota(I32, (LANES, LANES), 0)
 
-    @pl.loop(0, wgt.shape[0] // SUB)
+    @pl.loop(0, wgt.shape[0] // SUB, unroll=2)
     def _(group):
         base = pl.multiple_of(group * SUB, SUB)
         rows = pl.ds(base, SUB)
@@ -121,7 +121,7 @@
 
     lane = lax.broadcasted_iota(I32, (chunk, SUB, LANES), 2)
 
-    @pl.loop(0, span_y // chunk)
+    @pl.loop(0, span_y // chunk, unroll=2)
     def _(k):
         y = k * chunk
         rows = pl.ds(pl.multiple_of((x * span_y + y) * SUB, SUB), chunk * SUB)
@@ -260,7 +260,7 @@
     def layers(low, high, body):
         @pl.loop(low, high)
         def _(x):
-            @pl.loop(0, span_y // chunk)
+            @pl.loop(0, span_y // chunk, unroll=2)
             def _(k):
                 body(x, k * chunk)
 
@@ -384,7 +384,7 @@
 
 
 def gather_kernel(cap, vel, off, slot, back, out, stage):
-    @pl.loop(0, off.shape[0] // SUB)
+    @pl.loop(0, off.shape[0] // SUB, unroll=4)
     def _(group):
         base = pl.multiple_of(group * SUB, SUB)
         rows = pl.ds(base, SUB)

time: 216 us -> 208 us (0.963); the launches traced: 219 us -> 208 us
  Pallas kernels: 114 us -> 103 us
    pallas_call x1, Pallas kernels: 19.5 us -> 15.7 us  [on_device(): pl.pallas_call(functools.partial(splat_kernel, devices, cap), out_shape=(...]
    pallas_call x1, Pallas kernels: 8.39 us -> 4.82 us  [on_device(): pl.pallas_call(functools.partial(gather_kernel, cap), out_shape=struct((3...]
where the time goes in v4:
time: 208 us
  Pallas kernels  103 us (50%)
  waiting for transfers between devices  67.8 us (33%)
  starting transfers between devices  26.7 us (13%)
  local copies, waits for them, and re-layouts  4.62 us (2%)
  other arithmetic  4.54 us (2%)
    pallas_call x1, Pallas kernels, on_device(): pl.pallas_call(functools.partial(solve_kernel, devices, cap), out_shape=(...  55.9 us
    all_to_all x1, waiting for transfers between devices, on_device(): arrived = exchange(send.reshape(devices, stride, LANES))  25.4 us
    all_to_all x1, waiting for transfers between devices, on_device(): returned = exchange(reply.reshape(devices, 3 * cap, LANES))  24.6 us
    ppermute x2, waiting for transfers between devices, shifted(): return lax.ppermute(block, axis, route)  17.9 us
    all_to_all x1, starting transfers between devices, on_device(): returned = exchange(reply.reshape(devices, 3 * cap, LANES))  16.7 us
    pallas_call x1, Pallas kernels, on_device(): pl.pallas_call(functools.partial(splat_kernel, devices, cap), out_shape=(...  15.7 us
    pallas_call x1, Pallas kernels, on_device(): pl.pallas_call(functools.partial(grid_kernel, devices, cap), grid=(span_x...  13.8 us
    pallas_call x1, Pallas kernels, on_device(): pl.pallas_call(face_kernel, grid=(span_x,), out_shape=(struct((3,) + flag...  13.1 us
  transfers between devices with their start and end apart: 4, of which 4 were waited for; matrix products, arithmetic and copies ran while one was open for 3% of the time, Pallas kernels for 6%

profile of v4, /device:TPU:0, one launch (start us, length us, event | category | flops | bytes accessed | tf_op | source)
XLA Modules:
  0.0 207.8 jit_solution(9337121198049399491)
XLA Ops:
  0.6 15.7 %splat.1 = (f32[4352,128]{1,0:T(8,128)}, s32[512]{0:T(512)}) custom-call(f32[3,512,128]{2,1,0:T(8,128)} %bitcast.19, f32[512,128]{1,0:T(8,128)} %wgt.1, s32[512,128]{1,0:T(8,128)} %off.3, s32[512]{0:T(512)} %bitcast.24, s32[512]{0:T(512)} %bitcast.25), custom_call_target="tpu_custom_call" | custom-call | tf_op jit(solution)/shard_map/splat/pallas_call | solution.py:418
  16.3 7.3 %all-to-all-start = ((f32[32,136,128]{2,1,0:T(8,128)}), f32[32,136,128]{2,1,0:T(8,128)S(1)}, u32[]{:S(2)}, u32[]{:S(2)}) async-start(f32[32,136,128]{2,1,0:T(8,128)} %bitcast.21), calls=%async_computation | async-start | bytes 4456448 | tf_op jit(solution)/shard_map/all_to_all | solution.py:434
  23.7 2.0 fusion.2
  25.7 0.0 copy-start.1
  25.7 1.4 collective-permute-start
  27.2 1.3 collective-permute-start.1
  28.5 0.3 slice.27
  28.9 0.6 slice.29
  29.5 0.8 collective-permute-done.1
  30.3 17.1 %collective-permute-done = f32[1,64,1024]{2,1,0:T(8,128)S(1)} collective-permute-done((f32[1,64,1024]{2,1,0:T(8,128)S(1)}, f32[1,64,1024]{2,1,0:T(8,128)S(1)}, u32[]{:S(2)}, u32[]{:S(2)}) %collective-permute-start) | collective-permute-done | bytes 262176 | tf_op jit(solution)/shard_map/ppermute | solution.py:40
  47.5 0.0 copy-done.1
  47.5 1.2 select_add_fusion
  48.6 1.8 copy.9
  50.4 25.4 %all-to-all-done = f32[32,136,128]{2,1,0:T(8,128)S(1)} async-done(((f32[32,136,128]{2,1,0:T(8,128)}), f32[32,136,128]{2,1,0:T(8,128)S(1)}, u32[]{:S(2)}, u32[]{:S(2)}) %all-to-all-start) | async-done | bytes 2228256 | tf_op jit(solution)/shard_map/all_to_all | solution.py:434
  75.8 1.3 fusion
  77.1 0.7 convert_element_type.22.brick
  77.8 0.0 copy-done
  77.8 13.8 %grid.1 = (f32[3,8,64,8,128]{4,3,2,1,0:T(8,128)}, f32[3,8,64,8,128]{4,3,2,1,0:T(8,128)}, f32[8,64,8,128]{3,2,1,0:T(8,128)}, f32[64,8,128]{2,1,0:T(8,128)}, f32[8,1,8,128]{3,2,1,0:T(8,128)}) custom-call(f32[4352,128]{1,0:T(8,128)} %bitcast.16, s32[1024]{0:T(1024)} %convert_element_type.22.brick, s32[32]{0:T(128)} %get-tuple-element.25.count, ...), custom_call_target="tpu_custom_call" | custom-call | tf_op jit(solution)/shard_map/grid/pallas_call | solution.py:453
  91.5 55.9 %solve.1 = (f32[10,66,8,128]{3,2,1,0:T(8,128)}, f32[3072,128]{1,0:T(8,128)}) custom-call(f32[3,4096,128]{2,1,0:T(8,128)} %bitcast.13, f32[3,8,64,8,128]{4,3,2,1,0:T(8,128)} %get-tuple-element.17.r_hbm.r, f32[8,64,8,128]{3,2,1,0:T(8,128)} %get-tuple-element.18.d_hbm, s32[8,64,8,128]{3,2,1,0:T(8,128)} %bitcast.15, f32[64,8,128]{2,1,0:T(8,128)} %get-tuple-element.19.ex_hbm, ...), custom_call_target="tpu_custom_call" | custom-call | tf_op jit(solution)/shard_map/solve/pallas_call | solution.py:481
  147.5 16.7 %all-to-all-start.1 = ((f32[32,96,128]{2,1,0:T(8,128)}), f32[32,96,128]{2,1,0:T(8,128)S(1)}, u32[]{:S(2)}, u32[]{:S(2)}) async-start(f32[32,96,128]{2,1,0:T(8,128)} %bitcast.22), calls=%async_computation.1 | async-start | bytes 3145728 | tf_op jit(solution)/shard_map/all_to_all | solution.py:507
  164.2 13.1 %faces.1 = (f32[3,8,64,1024]{3,2,1,0:T(8,128)}, f32[8,64,1024]{2,1,0:T(8,128)}) custom-call(f32[3,8,64,8,128]{4,3,2,1,0:T(8,128)} %get-tuple-element.16.g, f32[3,8,64,8,128]{4,3,2,1,0:T(8,128)} %get-tuple-element.17.r_hbm.r, f32[10,66,8,128]{3,2,1,0:T(8,128)} %get-tuple-element.22.p_here.p_next, f32[10,66,8,128]{3,2,1,0:T(8,128)} %get-tuple-element.22.p_here.p_next), custom_call_target="tpu_custom_call" | custom-call | flops 10000000 | bytes 24000000 | tf_op jit(solution)/shard_map/faces/pallas_call | solution.py:509
  177.2 24.6 %all-to-all-done.1 = f32[32,96,128]{2,1,0:T(8,128)S(1)} async-done(((f32[32,96,128]{2,1,0:T(8,128)}), f32[32,96,128]{2,1,0:T(8,128)S(1)}, u32[]{:S(2)}, u32[]{:S(2)}) %all-to-all-start.1) | async-done | bytes 1572896 | tf_op jit(solution)/shard_map/all_to_all | solution.py:507
  201.8 1.1 copy-done.2
  202.9 4.8 %gather.1 = f32[3,512,128]{2,1,0:T(8,128)} custom-call(f32[3,512,128]{2,1,0:T(8,128)} %bitcast.20, s32[512,128]{1,0:T(8,128)} %off.3, s32[512]{0:T(512)} %get-tuple-element.14.slot, f32[3072,128]{1,0:T(8,128)} %bitcast.18), custom_call_target="tpu_custom_call" | custom-call | tf_op jit(solution)/shard_map/gather/pallas_call | solution.py:529
  (7 shorter events, 0.2 us)
Async XLA Ops:
  16.3 59.5 %all-to-all-start = ((f32[32,136,128]{2,1,0:T(8,128)}), f32[32,136,128]{2,1,0:T(8,128)S(1)}, u32[]{:S(2)}, u32[]{:S(2)}) async-start(f32[32,136,128]{2,1,0:T(8,128)} %bitcast.21), calls=%async_computation | async-start | bytes 4456448 | tf_op jit(solution)/shard_map/all_to_all | solution.py:434
  25.7 21.8 %copy-start.1 = (s32[8,64,1024]{2,1,0:T(8,128)S(1)}, s32[8,64,1024]{2,1,0:T(8,128)}, u32[]{:S(2)}) copy-start(s32[8,64,1024]{2,1,0:T(8,128)} %param.11) | copy-start | bytes 6291460
  25.7 21.7 %collective-permute-start = (f32[1,64,1024]{2,1,0:T(8,128)S(1)}, f32[1,64,1024]{2,1,0:T(8,128)S(1)}, u32[]{:S(2)}, u32[]{:S(2)}) collective-permute-start(f32[1,64,1024]{2,1,0:T(8,128)S(1)} %slice.26), channel_id=1, source_target_pairs={{4,0},{8,4},{12,8},{16,12},{20,16},{24,20},{28,24},{5,1},{9,5},{13... | collective-permute-start | bytes 786440 | tf_op jit(solution)/shard_map/ppermute | solution.py:40
  27.2 3.1 %collective-permute-start.1 = (f32[8,1,1024]{2,1,0:T(1,128)S(1)}, f32[8,1,1024]{2,1,0:T(1,128)S(1)}, u32[]{:S(2)}, u32[]{:S(2)}) collective-permute-start(f32[8,1,1024]{2,1,0:T(1,128)S(1)} %slice.28), channel_id=1, source_target_pairs={{1,0},{2,1},{3,2},{5,4},{6,5},{7,6},{9,8},{10,9},{11,10},{13,12},{... | collective-permute-start | bytes 98312 | tf_op jit(solution)/shard_map/ppermute | solution.py:40
  75.8 2.0 copy-start
  147.5 54.3 %all-to-all-start.1 = ((f32[32,96,128]{2,1,0:T(8,128)}), f32[32,96,128]{2,1,0:T(8,128)S(1)}, u32[]{:S(2)}, u32[]{:S(2)}) async-start(f32[32,96,128]{2,1,0:T(8,128)} %bitcast.22), calls=%async_computation.1 | async-start | bytes 3145728 | tf_op jit(solution)/shard_map/all_to_all | solution.py:507
  201.8 1.1 copy-start.2
